TPU v7x, 256 devices: a whole 4x4x8 slice. The times are simulated.
256 devices in a mesh: fsdp: 64 (over x, y_lo, z), tp: 4 (over y_hi, core).
Axes of the slice: x: 4, y: 4 (y_hi: 2, y_lo: 2; y = y_hi * 2 + y_lo), z: 8, core: 2. Of those that a mesh axis runs over, the one named last changes fastest.
Arguments:
- tokens: bfloat16 [8192, 4096], P('fsdp'), may hold values from -6 to 6
- gate_left: bfloat16 [4096, 1024], P('fsdp', 'tp'), may hold values from -0.09375 to 0.09375
- gate_right: bfloat16 [1024, 14336], P('fsdp', 'tp'), may hold values from -0.1875 to 0.1875
- gate_values: bfloat16 [108, 16384], P('tp', 'fsdp'), may hold values from -0.5 to 0.5
- gate_rows: int32 [108], P('tp'), may hold values from 0 to 31
- gate_cols: int32 [108], P('tp'), may hold values from 0 to 111, as said below
- up_left: bfloat16 [4096, 1024], P('fsdp', 'tp'), may hold values from -0.09375 to 0.09375
- up_right: bfloat16 [1024, 14336], P('fsdp', 'tp'), may hold values from -0.1875 to 0.1875
- up_values: bfloat16 [108, 16384], P('tp', 'fsdp'), may hold values from -0.5 to 0.5
- up_rows: int32 [108], P('tp'), may hold values from 0 to 31
- up_cols: int32 [108], P('tp'), may hold values from 0 to 111, as said below
- grad_hidden: bfloat16 [8192, 14336], P('fsdp', 'tp'), may hold values from -6 to 6
Outputs:
- hidden: bfloat16 [8192, 14336], P('fsdp', 'tp')
- grad_gate_values: float32 [108, 16384], P('tp', 'fsdp')
- grad_up_values: float32 [108, 16384], P('tp', 'fsdp')
Inputs may be any that keep to these rules, and one draw needn't show every extreme that they name: `gate_cols`: support blocks of one projection are distinct (row block, column block) pairs; the entries that lie on index t of tp have column blocks from t * 14336 // (128 * 4) to (t + 1) * 14336 // (128 * 4) - 1. Rows and columns of one projection go together. `up_cols`: as for the gate projection.
All inputs are finite; a program needn't handle non-finite values.
Results may differ from a plain program's by a relative error of at most 0.005.
Values may be sent and summed in bfloat16 or wider, within the bound.
A program may use at most 128 MiB of HBM per device.

v0:
```python
import jax
import jax.numpy as jnp
from jax import lax
from jax.sharding import Mesh
from jax.sharding import PartitionSpec as P

BLK = 128
FSDP = ("fsdp_0", "fsdp_1", "fsdp_2")


def side_by_side(arrays, axis, dim, along):
    both = jnp.concatenate(arrays, axis=along)
    result, at, gathered = (lax.all_gather(both, axis, axis=dim, tiled=True), 0, [])
    for a in arrays:
        gathered.append(lax.slice_in_dim(result, at, at + a.shape[along], axis=along))
        at += a.shape[along]
    return tuple(gathered)


def in_blocks(value, dim, length):
    before, after = (value.shape[:dim], value.shape[dim + 1 :])
    return jnp.moveaxis(value.reshape(*before, length, -1, *after), dim, 0)


def summed_on_arrival(value, axis, dim):
    length = lax.axis_size(axis)
    pieces = lax.all_to_all(in_blocks(value, dim, length), axis, 0, 0, tiled=True)
    return jnp.sum(pieces, axis=0)


def sum_by_axis(value, axes, dim):
    far, near = axes
    leading = summed_on_arrival(value, far, dim)
    return summed_on_arrival(leading, near, dim)


def in_one_piece(arrays, axis, dim, along):
    ends, at = ([], 0)
    for a in arrays[:-1]:
        at += a.shape[along]
        ends.append(at)
    both = jnp.concatenate(arrays, axis=along)
    return tuple(jnp.split(sum_by_axis(both, axis, dim), ends, axis=along))


def support_forward(tokens, blocks, rows, cols_local, col_blocks):
    width = tokens.shape[1] // BLK
    sources = tokens.reshape(tokens.shape[0], width, BLK)[:, rows, :]
    parts = jnp.einsum("tkb,kbc->tkc", sources, blocks, preferred_element_type=jnp.float32)
    placed = (
        jnp.zeros((tokens.shape[0], col_blocks, BLK), jnp.float32).at[:, cols_local, :].add(parts)
    )
    return (placed.reshape(tokens.shape[0], col_blocks * BLK), sources)


def value_terms(sources_gate, dpre_gate, local_gate, sources_up, dpre_up, local_up, col_blocks):
    picked_gate = dpre_gate.reshape(dpre_gate.shape[0], col_blocks, BLK)[:, local_gate, :]
    picked_up = dpre_up.reshape(dpre_up.shape[0], col_blocks, BLK)[:, local_up, :]
    value_gate = jnp.einsum(
        "tkb,tkc->kbc", sources_gate, picked_gate, preferred_element_type=jnp.float32
    )
    value_up = jnp.einsum("tkb,tkc->kbc", sources_up, picked_up, preferred_element_type=jnp.float32)
    return (
        value_gate.reshape(value_gate.shape[0], BLK * BLK),
        value_up.reshape(value_up.shape[0], BLK * BLK),
    )


def on_device(
    tokens,
    gate_left,
    gate_right,
    gate_values,
    gate_rows,
    gate_cols,
    up_left,
    up_right,
    up_values,
    up_rows,
    up_cols,
    grad_hidden,
):
    left_gate, left_up = side_by_side((gate_left, up_left), FSDP, 0, 1)
    rank_gate = jnp.dot(tokens, left_gate, preferred_element_type=jnp.float32).astype(jnp.bfloat16)
    rank_up = jnp.dot(tokens, left_up, preferred_element_type=jnp.float32).astype(jnp.bfloat16)
    full_gate, full_up = side_by_side((rank_gate, rank_up), "tp", 1, 0)
    flat_gate, flat_up = side_by_side((gate_values, up_values), FSDP, 1, 0)
    blocks_gate = flat_gate.reshape(flat_gate.shape[0], BLK, BLK)
    blocks_up = flat_up.reshape(flat_up.shape[0], BLK, BLK)
    right_gate, right_up = side_by_side((gate_right, up_right), FSDP, 0, 1)
    col_blocks = right_gate.shape[1] // BLK
    col_base = lax.axis_index("tp") * col_blocks
    local_gate = gate_cols - col_base
    local_up = up_cols - col_base
    sparse_gate, sources_gate = support_forward(
        tokens, blocks_gate, gate_rows, local_gate, col_blocks
    )
    sparse_up, sources_up = support_forward(tokens, blocks_up, up_rows, local_up, col_blocks)
    pre_gate = jnp.dot(full_gate, right_gate, preferred_element_type=jnp.float32) + sparse_gate
    pre_up = jnp.dot(full_up, right_up, preferred_element_type=jnp.float32) + sparse_up
    sigma = jax.nn.sigmoid(pre_gate)
    silu = pre_gate * sigma
    upstream = grad_hidden.astype(jnp.float32)
    dpre_gate = (upstream * pre_up * sigma * (1.0 + pre_gate * (1.0 - sigma))).astype(jnp.bfloat16)
    dpre_up = (upstream * silu).astype(jnp.bfloat16)
    hidden = (silu * pre_up).astype(jnp.bfloat16)
    value_gate, value_up = value_terms(
        sources_gate, dpre_gate, local_gate, sources_up, dpre_up, local_up, col_blocks
    )
    grad_gate_values, grad_up_values = in_one_piece(
        (value_gate, value_up), ("fsdp_0", ("fsdp_1", "fsdp_2")), 1, 0
    )
    return (hidden, grad_gate_values, grad_up_values)


def solution(mesh):
    finer = Mesh(
        mesh.devices.reshape(4, 2, 8, mesh.shape["tp"]), ("fsdp_0", "fsdp_1", "fsdp_2", "tp")
    )
    return jax.shard_map(
        on_device,
        mesh=finer,
        in_specs=(
            P(FSDP, None),
            P(FSDP, "tp"),
            P(FSDP, "tp"),
            P("tp", FSDP),
            P("tp"),
            P("tp"),
            P(FSDP, "tp"),
            P(FSDP, "tp"),
            P("tp", FSDP),
            P("tp"),
            P("tp"),
            P(FSDP, "tp"),
        ),
        out_specs=(P(FSDP, "tp"), P("tp", FSDP), P("tp", FSDP)),
        check_vma=False,
    )
```

profile of v0, /device:TPU:16, one launch (start us, length us, event | category | flops | bytes accessed | tf_op | source)
XLA Modules:
  0.0 966.0 jit_solution(18411357769990598574)
XLA Ops:
  7.2 1.4 pad_maximum_fusion.3
  8.6 1.4 pad_maximum_fusion.2
  10.1 1.7 pad_maximum_fusion
  11.8 1.6 copy.57
  14.2 1.7 gather_fusion
  16.7 229.1 %all-gather.8.cloned.1.call-done = bf16[54,16384]{1,0:T(8,128)(2,1)} async-done(((bf16[54,256]{1,0:T(8,128)(2,1)}), bf16[54,16384]{1,0:T(8,128)(2,1)}) %all-gather.8.cloned.1.call-update) | async-done | bytes 1769488 | tf_op jit(solution)/shard_map/all_gather | solution.py:13
  245.8 2.8 fusion.45
  249.7 1.6 fusion.33
  251.5 4.6 scatter_fusion
  256.1 1.7 copy.59
  257.8 2.8 copy.60
  260.9 1.6 fusion.31
  262.7 4.6 scatter_fusion.1
  267.3 1.7 copy.62
  269.0 2.8 copy.63
  271.8 276.9 %all-gather.4.cloned.1.call-done = bf16[4096,512]{1,0:T(8,128)(2,1)} async-done(((bf16[64,512]{1,0:T(8,128)(2,1)}), bf16[4096,512]{1,0:T(8,128)(2,1)}) %all-gather.4.cloned.1.call-update) | async-done | bytes 4194320 | tf_op jit(solution)/shard_map/all_gather | solution.py:13
  548.7 2.1 fusion.25
  550.9 2.2 fusion.28
  553.1 8.2 all_gather.13
  561.3 314.6 %all-gather.6.cloned.1.call-done = bf16[1024,7168]{1,0:T(8,128)(2,1)} async-done(((bf16[16,7168]{1,0:T(8,128)(2,1)}), bf16[1024,7168]{1,0:T(8,128)(2,1)}) %all-gather.6.cloned.1.call-update) | async-done | bytes 14680080 | tf_op jit(solution)/shard_map/all_gather | solution.py:13
  875.9 4.4 fusion.4
  880.3 6.2 fusion.16
  887.8 1.7 copy.65
  889.4 1.6 gather_fusion.2
  891.1 1.6 fusion.37
  892.7 1.8 concatenate.24
  894.5 3.9 copy.70
  900.9 1.8 concatenate.25
  902.6 2.7 copy.71
  905.7 28.3 %all_to_all.10 = f32[4,54,4096]{2,1,0:T(8,128)} all-to-all(f32[4,54,4096]{2,1,0:T(8,128)S(1)} %maximum_bitcast_fusion), channel_id=1, replica_groups=mesh['fsdp_0'=4,'fsdp_1'=2,'fsdp_2'=8,'tp'=4] {'fsdp_0'}, dimensions={0} | all-to-all | bytes 7077888 | tf_op jit(solution)/shard_map/all_to_all | solution.py:27
  934.0 2.3 reduce_sum.18
  937.3 21.5 %all_to_all.11 = f32[16,54,256]{2,1,0:T(8,128)S(1)} all-to-all(f32[16,54,256]{2,1,0:T(8,128)S(1)} %copy.72), channel_id=1, replica_groups=mesh['fsdp_0'=4,'fsdp_1'=2,'fsdp_2'=8,'tp'=4] {'fsdp_1','fsdp_2'}, dimensions={0} | all-to-all | bytes 1769472 | tf_op jit(solution)/shard_map/all_to_all | solution.py:27
  (59 shorter events, 9.1 us)
Async XLA Ops:
  7.2 238.6 %all-gather.8.cloned.1.call-start = ((), (), s32[]{:S(2)}) async-start(), calls=%async_computation.4 | async-start | bytes 1863680 | tf_op jit(solution)/shard_map/all_gather | solution.py:13
  8.6 540.1 %all-gather.4.cloned.1.call-start = ((), (), s32[]{:S(2)}) async-start(), calls=%async_computation.2 | async-start | bytes 4259840 | tf_op jit(solution)/shard_map/all_gather | solution.py:13
  10.1 865.8 %all-gather.6.cloned.1.call-start = ((), (), s32[]{:S(2)}) async-start(), calls=%async_computation.3 | async-start | bytes 14909440 | tf_op jit(solution)/shard_map/all_gather | solution.py:13
  11.8 2.3 copy-start.12
  13.4 2.4 copy-start.13
  14.2 2.4 copy-start.9
  14.2 2.4 copy-start.10
  248.5 1.2 copy-start
  257.8 2.8 copy-start.4
  268.9 279.8 %copy-start.6 = (bf16[128,4096]{1,0:T(8,128)(2,1)S(1)}, bf16[128,4096]{1,0:T(8,128)(2,1)}, u32[]{:S(2)}) copy-start(bf16[128,4096]{1,0:T(8,128)(2,1)} %param.12) | copy-start | bytes 3145732
  548.7 2.1 copy-start.7
  550.9 325.0 %copy-start.3 = (f32[128,3584]{1,0:T(8,128)S(1)}, f32[128,3584]{1,0:T(8,128)}, u32[]{:S(2)}) copy-start(f32[128,3584]{1,0:T(8,128)} %copy.60) | copy-start | bytes 5505028
  875.9 4.4 copy-start.5
  875.9 4.4 copy-start.11
  887.8 3.3 copy-start.1
  894.5 3.9 copy-start.8
  902.6 2.7 copy-start.2
Sparse Core Ops, SparseCore 0:
  10.3 235.4 all-gather.7
  247.6 301.1 all-gather.3
  551.1 324.7 all-gather.5
where the time goes:
time: 967 us; the launch traced here: 966 us
  waiting for transfers between devices  821 us (85%)
  blocking collectives  58 us (6%)
  local copies, waits for them, and re-layouts  36.5 us (4%)
  matrix products  20.2 us (2%)
  other arithmetic  16.4 us (2%)
  between operations  14.1 us (1%)
    all_gather x3, waiting for transfers between devices, side_by_side(): lax.all_gather(both, axis, axis=dim, tiled=True)  821 us
    all_to_all x2, blocking collectives, summed_on_arrival(): lax.all_to_all(in_blocks(value, dim, length), axis, 0, 0, tiled=True)  49.8 us
  transfers between devices with their start and end apart: 3, of which 3 were waited for; matrix products, arithmetic and copies ran while one was open for 4% of the time, Pallas kernels for 0%

commit v1 on v0

v1 whole, which is shorter than its diff:
```python
import heapq

import jax
import jax.numpy as jnp
from jax import lax
from jax.experimental import pallas as pl
from jax.experimental.pallas import tpu as pltpu
from jax.sharding import Mesh
from jax.sharding import PartitionSpec as P

BLK = 128
NX, NL, NZ, NH, NC = 4, 2, 8, 2, 2
FSDP = ("x", "yl", "z")
TP = ("yh", "c")
KB = 27
HALF = 1792
TILE = 256
PART_A = 768
ALL = slice(None)
F32, BF16 = jnp.float32, jnp.bfloat16


def dot(a, b):
    return jnp.dot(a, b, preferred_element_type=F32)


class Net:
    LATENCY = 1.5
    RATE = {"x+": 0.045, "x-": 0.045, "z+": 0.045, "z-": 0.045, "y": 0.045, "c": 0.2}

    def __init__(self, send_sems, recv_sems):
        self.sems = (send_sems, recv_sems)
        self.now, self.free, self.heap, self.copies, self.spare = 0.0, {}, [], [], []

    def copy(self, src, dst, where):
        i = len(self.copies)
        made = pltpu.make_async_remote_copy(
            src_ref=src,
            dst_ref=dst,
            send_sem=self.sems[0].at[i],
            recv_sem=self.sems[1].at[i],
            device_id=where,
            device_id_type=pl.DeviceIdType.MESH,
        )
        return made

    def track(self, made, link, size, then):
        self.copies.append(made)
        begin = max(self.now, self.free.get(link, 0.0))
        self.free[link] = begin + size / self.RATE[link]
        heapq.heappush(self.heap, (self.free[link] + self.LATENCY, len(self.copies), made, then))

    def send(self, src, dst, where, link, size, then):
        made = self.copy(src, dst, where)
        made.start()
        self.track(made, link, size, then)

    def work(self, cost, do):
        do()
        self.now += cost

    def run(self):
        while self.heap:
            at, _, made, then = heapq.heappop(self.heap)
            while self.spare and self.now + self.spare[0][0] <= at + 0.5:
                self.work(*self.spare.pop(0))
            self.now = max(self.now, at)
            made.wait_recv()
            then()
        while self.spare:
            self.work(*self.spare.pop(0))

    def finish(self):
        for made in self.copies:
            made.wait_send()


class Count:
    def __init__(self, n, then):
        self.n, self.then = n, then

    def __call__(self):
        self.n -= 1
        if self.n == 0:
            self.then()


def ring_gather(net, n, me, axis, block, size, done):
    reach = n // 2
    left_over = Count(2 * reach, done)

    def step(way, s):
        whose = lax.rem(me - way * (s - 1) + n, n)
        half = ALL if s < reach else (0 if way == 1 else 1)
        ref = block(whose, half)
        to = lax.rem(me + way + n, n)
        net.send(
            ref,
            ref,
            {axis: to},
            axis + ("+" if way == 1 else "-"),
            size if s < reach else size / 2,
            lambda: arrived(way, s),
        )

    def arrived(way, s):
        if s < reach:
            step(way, s + 1)
        left_over()

    step(1, 1)
    step(-1, 1)


def kernel(
    tok,
    gate_left,
    gate_right,
    gate_values,
    gate_rows,
    gate_cols,
    up_left,
    up_right,
    up_values,
    up_rows,
    up_cols,
    grad_hidden,
    table,
    hidden,
    out_gate,
    out_up,
    t_all,
    t_perm,
    t_turn,
    left,
    right,
    shards,
    blocks,
    rank,
    pre,
    chain,
    up_stream,
    dpre,
    back,
    grads,
    came_up,
    came_down,
    mine,
    parcels,
    arrived_parcels,
    send_sems,
    recv_sems,
    local_sems,
):
    x, yl, z = lax.axis_index("x"), lax.axis_index("yl"), lax.axis_index("z")
    yh, c = lax.axis_index("yh"), lax.axis_index("c")
    other = 1 - yl

    def round_x(d):
        return lax.rem(x + d + NX, NX)

    def round_z(d):
        return lax.rem(z + d + NZ, NZ)

    pair, twin = {"yl": other}, {"c": 1 - c}
    across, beyond = {"yh": 1 - yh}, {"yh": 1 - yh, "yl": other}
    near = [{"x": round_x(d), "yl": yl if e == 0 else other} for d in range(NX) for e in range(NL)][1:]
    greeted = [twin, across, beyond, {"z": round_z(1)}, {"z": round_z(-1)}, *near]
    barrier = pltpu.get_barrier_semaphore()
    for who in greeted:
        pl.semaphore_signal(barrier, inc=1, device_id=who, device_id_type=pl.DeviceIdType.MESH)

    keeps = []

    def keep(src, dst):
        made = pltpu.make_async_copy(src, dst, local_sems.at[len(keeps)])
        made.start()
        keeps.append(made)

    def cols(ref, which):
        return ref.at[:, pl.ds(pl.multiple_of(which * HALF, BLK), HALF)]

    own_rows = pl.ds(pl.multiple_of(yl * BLK, BLK), BLK)
    other_rows = pl.ds(pl.multiple_of(other * BLK, BLK), BLK)
    keep(cols(gate_right, yl), right.at[x, yl, z, :, 0:HALF])
    keep(cols(up_right, yl), right.at[x, yl, z, :, HALF : 2 * HALF])
    keep(tok, t_all.at[own_rows])
    keep(cols(grad_hidden, yl), up_stream.at[own_rows])
    own_left = pltpu.make_async_copy(gate_left, left.at[x, yl, z], local_sems.at[len(keeps)])

    @pl.when(yl == 0)
    def _():
        own_left.start()

    @pl.when(yl == 1)
    def _():
        pltpu.make_async_copy(up_left, left.at[x, yl, z], local_sems.at[len(keeps)]).start()

    keeps.append(own_left)
    shards[x, yl] = jnp.zeros((2, 32, 2 * BLK), BF16)
    shards[x, yl, 0, 0:KB] = gate_values[...]
    shards[x, yl, 1, 0:KB] = up_values[...]

    pl.semaphore_wait(barrier, len(greeted))
    net = Net(send_sems, recv_sems)

    def do_rank():
        total = jnp.zeros((2 * BLK, TILE), F32)
        for i in range(NX):
            total += dot(t_all[:, i * 1024 : (i + 1) * 1024], left[i].reshape(1024, TILE))
        slot = yl * 4 + yh * 2 + c
        rank[slot] = total.astype(BF16)

    def rank_slot(l, h, core):
        return rank.at[l * 4 + h * 2 + core]

    def share_rank():
        def on(l, h):
            ref = rank_slot(l, h, c)
            net.send(ref, ref, twin, "c", 0.131, rank_there)

        ref = rank_slot(yl, yh, c)
        net.send(ref, ref, pair, "y", 0.131, lambda: on(other, yh))
        net.send(ref, ref, beyond, "y", 0.0, lambda: on(other, 1 - yh))
        net.send(ref, ref, across, "y", 0.0, lambda: on(yl, 1 - yh))
        on(yl, yh)

    def low_rank(first, last):
        def do(j, _):
            g = (j >= 7).astype(jnp.int32)
            at = pl.ds(pl.multiple_of(j * TILE, TILE), TILE)
            total = jnp.zeros((2 * BLK, TILE), F32)
            for i in range(NX):
                total += dot(rank[g * 4 + i], right[i, :, :, :, at].reshape(TILE, TILE))
            pre[j] = total
            return 0

        lax.fori_loop(first, last, do, 0)

    tiles_a, tiles = PART_A // TILE, 2 * HALF // TILE
    product_a = Count(2, lambda: net.work(1.5, lambda: low_rank(0, tiles_a)))
    product_b = Count(2, lambda: net.work(5.0, lambda: low_rank(tiles_a, tiles)))

    def all_ranks():
        product_a()
        product_b()

    rank_there = Count(7 - 3, all_ranks)

    def rank_ready():
        net.work(2.5, do_rank)
        share_rank()

    left_parts = Count(2 + 1, rank_ready)

    def permute_tokens(first, last):
        def do(r, _):
            part = t_all[:, pl.ds(pl.multiple_of(r * BLK, BLK), BLK)]
            new = lax.broadcasted_iota(jnp.int32, (BLK, BLK), 0)
            old = lax.broadcasted_iota(jnp.int32, (BLK, BLK), 1)

            def source(m):
                shard = ((m >> 1) & 3) * 16 + (m & 1) * 8 + (m >> 4)
                return shard * 2 + ((m >> 3) & 1)

            turn = (source(new) == old).astype(F32).astype(BF16)
            straight = (source(old) == new).astype(F32).astype(BF16)
            t_perm[r] = dot(part, straight).astype(BF16)
            t_turn[r] = lax.dot_general(
                turn, part, (((1,), (1,)), ((), ())), preferred_element_type=F32
            ).astype(BF16)
            return 0

        lax.fori_loop(first, last, do, 0)

    def sparse(g, rows_ref, first, last):
        def do(k, _):
            piece = dot(t_perm[rows_ref[k]], blocks[g * KB + k])
            chain[g * 28 + k + 1] = piece + chain[g * 28 + table[g * 64 + k]]
            return 0

        lax.fori_loop(first, last, do, 0)

    def zero_chain():
        chain[0] = jnp.zeros((2 * BLK, BLK), F32)
        chain[28] = jnp.zeros((2 * BLK, BLK), F32)

    def all_sparse():
        net.spare.append((0.2, zero_chain))
        for g, rows_ref in ((0, gate_rows), (1, up_rows)):
            for first in range(0, KB, 9):
                net.spare.append((2.0, lambda a=(g, rows_ref, first, first + 9): sparse(*a)))

    sparse_ready = Count(2, all_sparse)

    def tokens_there():
        left_parts()
        for first in range(0, 32, 8):
            net.spare.append((1.2, lambda a=(first, first + 8): permute_tokens(*a)))
        sparse_ready()

    def spread_values():
        row = lax.broadcasted_iota(jnp.int32, (KB * 16, 512), 0)
        col = lax.broadcasted_iota(jnp.int32, (KB * 16, 512), 1)
        pick = col == (((row >> 3) & 1) * 256 + (row & 7) * 32 + (row >> 4))
        pick = pick.astype(F32).astype(BF16)
        for g in range(2):
            flat = shards[:, :, g].reshape(256, 2 * BLK)
            tall = jnp.concatenate([flat[:, :BLK], flat[:, BLK:]], axis=0)
            laid = dot(pick, tall).astype(BF16).reshape(KB, 16, BLK)
            blocks[g * KB : (g + 1) * KB, pl.ds(pl.multiple_of(z * 16, 16), 16), :] = laid

    def value_slice(i, half):
        some = {0: slice(0, KB), 1: slice(KB, 2 * KB)}.get(half if isinstance(half, int) else None, ALL)
        return blocks.at[some, pl.ds(pl.multiple_of(i * 16, 16), 16), :]

    def values_near():
        net.work(1.5, spread_values)
        ring_gather(net, NZ, z, "z", value_slice, 0.221, sparse_ready)

    def gather_left():
        a, b = slice(0, 32), slice(32, 64)

        def a_far():
            ring_gather(net, NZ, z, "z", lambda i, h: left.at[:, h, i, a], 0.131, left_parts)

        def b_far():
            ring_gather(net, NX, x, "x", lambda i, h: left.at[i, h, :, b], 0.262, left_parts)

        ring_gather(net, NX, x, "x", lambda i, h: left.at[i, h, z, a], 0.033, a_far)
        ring_gather(net, NZ, z, "z", lambda i, h: left.at[x, h, i, b], 0.033, b_far)

    def gather_right():
        a, b = slice(0, PART_A), slice(PART_A, 2 * HALF)
        size_a, size_b = PART_A * 64e-6, (2 * HALF - PART_A) * 64e-6

        def a_far():
            ring_gather(net, NZ, z, "z", lambda i, h: right.at[:, h, i, :, a], 4 * size_a, product_a)

        def b_far():
            ring_gather(net, NX, x, "x", lambda i, h: right.at[i, h, :, :, b], 8 * size_b, product_b)

        ring_gather(net, NX, x, "x", lambda i, h: right.at[i, h, z, :, a], size_a, a_far)
        ring_gather(net, NZ, z, "z", lambda i, h: right.at[x, h, i, :, b], size_b, b_far)

    swap_left = net.copy(up_left, left.at[x, yl, z], pair)

    @pl.when(yl == 0)
    def _():
        swap_left.start()

    @pl.when(yl == 1)
    def _():
        net.copy(gate_left, left.at[x, yl, z], pair).start()

    for made in keeps:
        made.wait()
    net.track(swap_left, "y", 0.033, gather_left)
    swapped_right = Count(2, gather_right)
    net.send(cols(gate_right, other), right.at[x, yl, z, :, 0:HALF], pair, "y", 0.057, swapped_right)
    net.send(
        cols(up_right, other), right.at[x, yl, z, :, HALF : 2 * HALF], pair, "y", 0.057, swapped_right
    )
    net.send(
        shards.at[x, yl],
        shards.at[x, yl],
        pair,
        "y",
        0.033,
        lambda: ring_gather(net, NX, x, "x", lambda i, h: shards.at[i, h], 0.066, values_near),
    )
    mine_half = pl.ds(pl.multiple_of(c * 64, 64), 64)
    sent_half = pl.ds(pl.multiple_of(yl * BLK + c * 64, 64), 64)
    got_half = pl.ds(pl.multiple_of(other * BLK + c * 64, 64), 64)
    net.send(
        tok.at[mine_half],
        t_all.at[sent_half],
        pair,
        "y",
        0.524,
        lambda: net.send(t_all.at[got_half], t_all.at[got_half], twin, "c", 0.524, tokens_there),
    )
    net.send(cols(grad_hidden, other), up_stream.at[own_rows], pair, "y", 0.459, lambda: None)
    net.run()

    def gated(j, _):
        for h in range(2):
            for rows, mine_too in ((other_rows, False), (own_rows, True)):
                lanes = slice(h * BLK, (h + 1) * BLK)
                col = j * 2 + h
                gate = pre[j, rows, lanes] + chain[table[32 + yl * 14 + col], rows, :]
                up = pre[7 + j, rows, lanes] + chain[28 + table[96 + yl * 14 + col], rows, :]
                coming = up_stream[rows, pl.ds(pl.multiple_of(col * BLK, BLK), BLK)].astype(F32)
                sigma = jax.nn.sigmoid(gate)
                silu = gate * sigma
                unit = (silu * up).astype(BF16)
                dpre[col, rows, :] = (coming * up * sigma * (1.0 + gate * (1.0 - sigma))).astype(BF16)
                dpre[14 + col, rows, :] = (coming * silu).astype(BF16)
                if mine_too:
                    hidden[:, pl.ds(pl.multiple_of(yl * HALF + col * BLK, BLK), BLK)] = unit
                else:
                    back[:, pl.ds(pl.multiple_of(col * BLK, BLK), BLK)] = unit
        return 0

    lax.fori_loop(0, 7, gated, 0)
    net.send(back, cols(hidden, yl), pair, "y", 0.459, lambda: None)

    for g, rows_ref, cols_ref in ((0, gate_rows, gate_cols), (1, up_rows, up_cols)):

        def gradient(k, _, g=g, rows_ref=rows_ref, cols_ref=cols_ref):
            col = cols_ref[k] - (yh * 2 + c) * 28 - yl * 14
            inside = (col >= 0) & (col < 14)
            term = dot(t_turn[rows_ref[k]], dpre[g * 14 + jnp.clip(col, 0, 13)])
            grads[g * KB + k] = jnp.where(inside, term, 0.0)
            return 0

        lax.fori_loop(0, KB, gradient, 0)

    def lot(i, part=16, skip=0):
        return pl.ds(pl.multiple_of(i * 16 + skip, 8), part)

    def exchange():
        mine[...] = (grads[:, lot(z), :] + came_up[3] + came_down[3]).reshape(2 * KB * 16, BLK)
        for s in range(8):
            for g in range(2):
                for p in range(2):
                    rows = pl.ds(g * KB * 16 + p * 8 + s, KB, stride=16)
                    parcels[s, g * 32 : g * 32 + KB, p * BLK : (p + 1) * BLK] = mine[rows, :]
        for d in range(NX):
            for e in range(NL):
                if d == 0 and e == 0:
                    continue
                to_x, to_l = round_x(d), (yl if e == 0 else other)
                net.send(
                    parcels.at[to_x * 2 + to_l],
                    arrived_parcels.at[d * 2 + e],
                    {"x": to_x, "yl": to_l},
                    "x+",
                    0.065,
                    lambda: None,
                )

    home = Count(2, exchange)

    def pass_on(way, j):
        buf = came_up if way == 1 else came_down
        whose = round_z(way * (5 - j))
        if j == 1:
            skip = 0 if way == 1 else 8
            src = grads.at[:, lot(whose, 8, skip), :]
            dst = buf.at[0, :, 0:8]
        else:
            src, dst = grads.at[:, lot(whose), :], buf.at[j - 1]
        net.send(
            src,
            dst,
            {"z": round_z(way)},
            "z+" if way == 1 else "z-",
            0.221 if j == 1 else 0.442,
            lambda: summed(way, j),
        )

    def summed(way, j):
        buf = came_up if way == 1 else came_down
        if j == 4:
            home()
            return
        whose = round_z(way * (4 - j))
        if j == 1:
            at = lot(whose, 8, 0 if way == 1 else 8)
            grads[:, at, :] = grads[:, at, :] + buf[0, :, 0:8, :]
        else:
            at = lot(whose)
            grads[:, at, :] = grads[:, at, :] + buf[j - 1]
        pass_on(way, j + 1)

    pass_on(1, 1)
    pass_on(-1, 1)
    net.run()
    total = parcels[x * 2 + yl]
    for i in range(1, 8):
        total = total + arrived_parcels[i]
    out_gate[...] = total[0:KB]
    out_up[...] = total[32 : 32 + KB]
    net.finish()


def chains(gate_cols, up_cols, base):
    cols = jnp.stack([gate_cols, up_cols]) - base
    index = jnp.arange(64, dtype=jnp.int32)
    padded = jnp.pad(cols, ((0, 0), (0, 64 - KB)))
    asked = jnp.where(index < 32, padded, index - 32)
    limit = jnp.where(index < 32, index, KB)
    earlier = jnp.arange(KB, dtype=jnp.int32)
    hit = (cols[:, None, :] == asked[:, :, None]) & (earlier < limit[:, None])
    return jnp.max(jnp.where(hit, earlier + 1, 0), axis=2).reshape(128)


def on_device(*args):
    base = (lax.axis_index("yh") * 2 + lax.axis_index("c")) * 28
    table = chains(args[5], args[10], base)
    vmem, smem = pl.BlockSpec(memory_space=pltpu.VMEM), pl.BlockSpec(memory_space=pltpu.SMEM)
    specs = [vmem, vmem, vmem, vmem, smem, smem, vmem, vmem, vmem, smem, smem, vmem, smem]
    copies = 110
    return pl.pallas_call(
        kernel,
        out_shape=(
            jax.ShapeDtypeStruct((BLK, 2 * HALF), BF16),
            jax.ShapeDtypeStruct((KB, 2 * BLK), F32),
            jax.ShapeDtypeStruct((KB, 2 * BLK), F32),
        ),
        in_specs=specs,
        out_specs=(vmem, vmem, vmem),
        scratch_shapes=[
            pltpu.VMEM((2 * BLK, 4096), BF16),
            pltpu.VMEM((32, 2 * BLK, BLK), BF16),
            pltpu.VMEM((32, BLK, 2 * BLK), BF16),
            pltpu.VMEM((NX, NL, NZ, 64, TILE), BF16),
            pltpu.VMEM((NX, NL, NZ, 16, 2 * HALF), BF16),
            pltpu.VMEM((NX, NL, 2, 32, 2 * BLK), BF16),
            pltpu.VMEM((2 * KB, BLK, BLK), BF16),
            pltpu.VMEM((8, 2 * BLK, TILE), BF16),
            pltpu.VMEM((14, 2 * BLK, TILE), F32),
            pltpu.VMEM((56, 2 * BLK, BLK), F32),
            pltpu.VMEM((2 * BLK, HALF), BF16),
            pltpu.VMEM((28, 2 * BLK, BLK), BF16),
            pltpu.VMEM((BLK, HALF), BF16),
            pltpu.VMEM((2 * KB, BLK, BLK), F32),
            pltpu.VMEM((4, 2 * KB, 16, BLK), F32),
            pltpu.VMEM((4, 2 * KB, 16, BLK), F32),
            pltpu.VMEM((2 * KB * 16, BLK), F32),
            pltpu.VMEM((8, 64, 2 * BLK), F32),
            pltpu.VMEM((8, 64, 2 * BLK), F32),
            pltpu.SemaphoreType.DMA((copies,)),
            pltpu.SemaphoreType.DMA((copies,)),
            pltpu.SemaphoreType.DMA((8,)),
        ],
        compiler_params=pltpu.CompilerParams(
            collective_id=0, has_side_effects=True, vmem_limit_bytes=58 * 2**20
        ),
    )(*args, table)


def solution(mesh):
    finer = Mesh(mesh.devices.reshape(NX, NL, NZ, NH, NC), (*FSDP, *TP))
    return jax.shard_map(
        on_device,
        mesh=finer,
        in_specs=(
            P(FSDP, None),
            P(FSDP, TP),
            P(FSDP, TP),
            P(TP, FSDP),
            P(TP),
            P(TP),
            P(FSDP, TP),
            P(FSDP, TP),
            P(TP, FSDP),
            P(TP),
            P(TP),
            P(FSDP, TP),
        ),
        out_specs=(P(FSDP, TP), P(TP, FSDP), P(TP, FSDP)),
        check_vma=False,
    )
```

time: 967 us -> 176 us (0.18)
  waiting for transfers between devices: 821 us -> 0 us
  Pallas kernels: 0 us -> 169 us
  blocking collectives: 58 us -> 0 us
  local copies, waits for them, and re-layouts: 36.5 us -> 4.91 us
  matrix products: 20.2 us -> 0 us
  other arithmetic: 16.4 us -> 0.17 us
  between operations: 14.1 us -> 0.71 us
    all_gather x3 -> x0, waiting for transfers between devices: 821 us -> none  [side_by_side(): lax.all_gather(both, axis, axis=dim, tiled=True)]
    pallas_call x0 -> x1, Pallas kernels: none -> 169 us  [on_device(): pl.pallas_call(kernel, out_shape=(jax.ShapeDtypeStruct((BLK, 2 * HALF), B...]
    all_to_all x2 -> x0, blocking collectives: 49.8 us -> none  [summed_on_arrival(): lax.all_to_all(in_blocks(value, dim, length), axis, 0, 0, tiled=True)]
    dot_general x8 -> x0, matrix products: 20.2 us -> none  [the longest x1 6.19 us: on_device(): jnp.dot(full_up, right_up, preferred_element_type=jnp.float32) + sparse_up]
    concatenate x4 -> x0, local copies, waits for them, and re-layouts: 10.1 us -> none  [in_one_piece(): both = jnp.concatenate(arrays, axis=along)]
  transfers between devices with their start and end apart: 3 -> 0, of which waited for: 3 -> 0; matrix products, arithmetic and copies ran while one was open for 4% -> 0% of each run, Pallas kernels for 0% -> 0%
where the time goes in v1:
time: 176 us; the launch traced here: 175 us
  Pallas kernels  169 us (96%)
  local copies, waits for them, and re-layouts  4.91 us (3%)
    pallas_call x1, Pallas kernels, on_device(): pl.pallas_call(kernel, out_shape=(jax.ShapeDtypeStruct((BLK, 2 * HALF), B...  169 us
    unnamed x11, local copies, waits for them, and re-layouts  4.21 us

profile of v1, /device:TPU:16, one launch (start us, length us, event | category | flops | bytes accessed | tf_op | source)
XLA Modules:
  0.0 175.2 jit_solution(8987315772298123839)
XLA Ops:
  0.6 0.0 copy-start.2
  0.6 0.0 copy-start.3
  0.7 0.6 copy-done.2
  1.3 0.0 copy-done.3
  1.4 0.1 copy.15
  1.5 0.1 fusion
  1.6 0.6 reshape.52.table
  2.2 169.4 %shard_map.139 = (bf16[128,3584]{1,0:T(8,128)(2,1)}, f32[27,256]{1,0:T(8,128)}, f32[27,256]{1,0:T(8,128)}) custom-call(bf16[128,4096]{1,0:T(8,128)(2,1)} %tok.1, bf16[64,256]{1,0:T(8,128)(2,1)} %gate_left.1, bf16[16,3584]{1,0:T(8,128)(2,1)} %gate_right.1, bf16[27,256]{1,0:T(8,128)(2,1)} %gate_values.1, s32[27]{0:T(128)} %gate_rows.1, s32[27]{0:T(128)} %gate_cols.1, ...), custom_call_target="tpu_custom_call" | custom-call | tf_op jit(solution)/shard_map/pallas_call | solution.py:505
  171.6 0.0 copy-start.1
  171.7 2.2 %copy.19 = bf16[128,3584]{1,0:T(8,128)(2,1)} copy(bf16[128,3584]{1,0:T(8,128)(2,1)} %get-tuple-element.6) | data formatting | bytes 1835008
  173.8 0.0 copy-done.1
  173.8 0.0 copy-start
  173.8 0.6 copy.20
  174.4 0.2 copy-done
  174.6 0.6 copy.21
  (7 shorter events, 0.0 us)
Async XLA Ops:
  0.6 0.7 copy-start.2
  0.6 0.7 copy-start.3
  171.6 2.2 %copy-start.1 = (f32[27,256]{1,0:T(8,128)S(1)}, f32[27,256]{1,0:T(8,128)}, u32[]{:S(2)}) copy-start(f32[27,256]{1,0:T(8,128)} %get-tuple-element.7) | copy-start | bytes 82948
  173.8 0.8 copy-start

commit v2 on v1

--- a/solution.py
+++ b/solution.py
@@ -25,7 +25,7 @@
 
 
 class Net:
-    LATENCY = 1.5
+    LATENCY = 3.0
     RATE = {"x+": 0.045, "x-": 0.045, "z+": 0.045, "z-": 0.045, "y": 0.045, "c": 0.2}
 
     def __init__(self, send_sems, recv_sems):
@@ -85,31 +85,29 @@
             self.then()
 
 
-def ring_gather(net, n, me, axis, block, size, done):
+def ring(net, n, me, axis, block, size, landed, far):
     reach = n // 2
-    left_over = Count(2 * reach, done)
 
     def step(way, s):
-        whose = lax.rem(me - way * (s - 1) + n, n)
-        half = ALL if s < reach else (0 if way == 1 else 1)
-        ref = block(whose, half)
+        part, share = (ALL, 1.0) if s < reach else far[way]
+        if part is None:
+            return
+        ref = block(lax.rem(me - way * (s - 1) + n, n), part)
         to = lax.rem(me + way + n, n)
-        net.send(
-            ref,
-            ref,
-            {axis: to},
-            axis + ("+" if way == 1 else "-"),
-            size if s < reach else size / 2,
-            lambda: arrived(way, s),
-        )
+        net.send(ref, ref, {axis: to}, axis + ("+" if way == 1 else "-"), size * share, lambda: arrived(way, s))
 
     def arrived(way, s):
         if s < reach:
             step(way, s + 1)
-        left_over()
+        landed((n - way * s) % n)
 
     step(1, 1)
     step(-1, 1)
+
+
+def ring_gather(net, n, me, axis, block, size, done):
+    count = Count(n, done)
+    ring(net, n, me, axis, block, size, lambda d: count(), {1: (0, 0.5), -1: (1, 0.5)})
 
 
 def kernel(
@@ -145,6 +143,8 @@
     grads,
     came_up,
     came_down,
+    leave_up,
+    leave_down,
     mine,
     parcels,
     arrived_parcels,
@@ -318,7 +318,22 @@
         net.work(1.5, spread_values)
         ring_gather(net, NZ, z, "z", value_slice, 0.221, sparse_ready)
 
-    def gather_left():
+    def gather(near_a, near_b, far_a, far_b):
+        counts_a = [Count(2, lambda d=d: far_a(d)) for d in range(NX)]
+        counts_b = [Count(2, lambda d=d: far_b(d)) for d in range(NZ)]
+
+        def begin(half, way):
+            far = {way: (ALL, 1.0), -way: (None, 0.0)}
+            ref_a, size_a = near_a
+            ref_b, size_b = near_b
+            ring(net, NX, x, "x", lambda i, _: ref_a(i, half), size_a, lambda d: counts_a[d](), far)
+            ring(net, NZ, z, "z", lambda i, _: ref_b(i, half), size_b, lambda d: counts_b[d](), far)
+            counts_a[0]()
+            counts_b[0]()
+
+        return (lambda: begin(yl, 1)), (lambda: begin(other, -1))
+
+    def left_gather():
         a, b = slice(0, 32), slice(32, 64)
 
         def a_far():
@@ -327,21 +342,33 @@
         def b_far():
             ring_gather(net, NX, x, "x", lambda i, h: left.at[i, h, :, b], 0.262, left_parts)
 
-        ring_gather(net, NX, x, "x", lambda i, h: left.at[i, h, z, a], 0.033, a_far)
-        ring_gather(net, NZ, z, "z", lambda i, h: left.at[x, h, i, b], 0.033, b_far)
-
-    def gather_right():
+        all_a, all_b = Count(NX, a_far), Count(NZ, b_far)
+        return gather(
+            (lambda i, h: left.at[i, h, z, a], 0.016),
+            (lambda i, h: left.at[x, h, i, b], 0.016),
+            lambda d: all_a(),
+            lambda d: all_b(),
+        )
+
+    def right_gather():
         a, b = slice(0, PART_A), slice(PART_A, 2 * HALF)
         size_a, size_b = PART_A * 64e-6, (2 * HALF - PART_A) * 64e-6
-
-        def a_far():
-            ring_gather(net, NZ, z, "z", lambda i, h: right.at[:, h, i, :, a], 4 * size_a, product_a)
-
-        def b_far():
-            ring_gather(net, NX, x, "x", lambda i, h: right.at[i, h, :, :, b], 8 * size_b, product_b)
-
-        ring_gather(net, NX, x, "x", lambda i, h: right.at[i, h, z, :, a], size_a, a_far)
-        ring_gather(net, NZ, z, "z", lambda i, h: right.at[x, h, i, :, b], size_b, b_far)
+        all_a, all_b = Count(NX, product_a), Count(NZ, product_b)
+
+        def a_far(d):
+            i = round_x(d)
+            ring_gather(net, NZ, z, "z", lambda k, h: right.at[i, h, k, :, a], size_a, all_a)
+
+        def b_far(d):
+            i = round_z(d)
+            ring_gather(net, NX, x, "x", lambda k, h: right.at[k, h, i, :, b], size_b, all_b)
+
+        return gather(
+            (lambda i, h: right.at[i, h, z, :, a], size_a / 2),
+            (lambda i, h: right.at[x, h, i, :, b], size_b / 2),
+            a_far,
+            b_far,
+        )
 
     swap_left = net.copy(up_left, left.at[x, yl, z], pair)
 
@@ -355,8 +382,10 @@
 
     for made in keeps:
         made.wait()
-    net.track(swap_left, "y", 0.033, gather_left)
-    swapped_right = Count(2, gather_right)
+    left_own, left_other = left_gather()
+    right_own, right_other = right_gather()
+    net.track(swap_left, "y", 0.033, left_other)
+    swapped_right = Count(2, right_other)
     net.send(cols(gate_right, other), right.at[x, yl, z, :, 0:HALF], pair, "y", 0.057, swapped_right)
     net.send(
         cols(up_right, other), right.at[x, yl, z, :, HALF : 2 * HALF], pair, "y", 0.057, swapped_right
@@ -381,6 +410,8 @@
         lambda: net.send(t_all.at[got_half], t_all.at[got_half], twin, "c", 0.524, tokens_there),
     )
     net.send(cols(grad_hidden, other), up_stream.at[own_rows], pair, "y", 0.459, lambda: None)
+    left_own()
+    right_own()
     net.run()
 
     def gated(j, _):
@@ -416,11 +447,12 @@
 
         lax.fori_loop(0, KB, gradient, 0)
 
-    def lot(i, part=16, skip=0):
-        return pl.ds(pl.multiple_of(i * 16 + skip, 8), part)
+    def lot(i):
+        return pl.ds(pl.multiple_of(i * 16, 16), 16)
 
     def exchange():
-        mine[...] = (grads[:, lot(z), :] + came_up[3] + came_down[3]).reshape(2 * KB * 16, BLK)
+        total = grads[:, lot(z), :] + came_up[3].astype(F32) + came_down[3].astype(F32)
+        mine[...] = total.reshape(2 * KB * 16, BLK)
         for s in range(8):
             for g in range(2):
                 for p in range(2):
@@ -443,36 +475,25 @@
     home = Count(2, exchange)
 
     def pass_on(way, j):
-        buf = came_up if way == 1 else came_down
-        whose = round_z(way * (5 - j))
-        if j == 1:
-            skip = 0 if way == 1 else 8
-            src = grads.at[:, lot(whose, 8, skip), :]
-            dst = buf.at[0, :, 0:8]
+        came, leaves = (came_up, leave_up) if way == 1 else (came_down, leave_down)
+        at = lot(round_z(way * (5 - j)))
+        first, last = (0, 2 * KB) if j > 1 else ((0, KB) if way == 1 else (KB, 2 * KB))
+        if j == 2:
+            half, rest = (slice(0, KB), slice(KB, 2 * KB))[::way]
+            leaves[1, half] = (grads[half, at, :] + came[0, half].astype(F32)).astype(BF16)
+            leaves[1, rest] = grads[rest, at, :].astype(BF16)
+        elif j > 2:
+            leaves[j - 1] = (grads[:, at, :] + came[j - 2].astype(F32)).astype(BF16)
         else:
-            src, dst = grads.at[:, lot(whose), :], buf.at[j - 1]
+            leaves[0, first:last] = grads[first:last, at, :].astype(BF16)
         net.send(
-            src,
-            dst,
+            leaves.at[j - 1, first:last],
+            came.at[j - 1, first:last],
             {"z": round_z(way)},
             "z+" if way == 1 else "z-",
-            0.221 if j == 1 else 0.442,
-            lambda: summed(way, j),
+            0.11 if j == 1 else 0.221,
+            lambda: home() if j == 4 else pass_on(way, j + 1),
         )
-
-    def summed(way, j):
-        buf = came_up if way == 1 else came_down
-        if j == 4:
-            home()
-            return
-        whose = round_z(way * (4 - j))
-        if j == 1:
-            at = lot(whose, 8, 0 if way == 1 else 8)
-            grads[:, at, :] = grads[:, at, :] + buf[0, :, 0:8, :]
-        else:
-            at = lot(whose)
-            grads[:, at, :] = grads[:, at, :] + buf[j - 1]
-        pass_on(way, j + 1)
 
     pass_on(1, 1)
     pass_on(-1, 1)
@@ -501,7 +522,7 @@
     table = chains(args[5], args[10], base)
     vmem, smem = pl.BlockSpec(memory_space=pltpu.VMEM), pl.BlockSpec(memory_space=pltpu.SMEM)
     specs = [vmem, vmem, vmem, vmem, smem, smem, vmem, vmem, vmem, smem, smem, vmem, smem]
-    copies = 110
+    copies = 176
     return pl.pallas_call(
         kernel,
         out_shape=(
@@ -526,8 +547,10 @@
             pltpu.VMEM((28, 2 * BLK, BLK), BF16),
             pltpu.VMEM((BLK, HALF), BF16),
             pltpu.VMEM((2 * KB, BLK, BLK), F32),
-            pltpu.VMEM((4, 2 * KB, 16, BLK), F32),
-            pltpu.VMEM((4, 2 * KB, 16, BLK), F32),
+            pltpu.VMEM((4, 2 * KB, 16, BLK), BF16),
+            pltpu.VMEM((4, 2 * KB, 16, BLK), BF16),
+            pltpu.VMEM((4, 2 * KB, 16, BLK), BF16),
+            pltpu.VMEM((4, 2 * KB, 16, BLK), BF16),
             pltpu.VMEM((2 * KB * 16, BLK), F32),
             pltpu.VMEM((8, 64, 2 * BLK), F32),
             pltpu.VMEM((8, 64, 2 * BLK), F32),

time: 176 us -> 140 us (0.80)
  Pallas kernels: 169 us -> 133 us
    pallas_call x1, Pallas kernels: 169 us -> 133 us  [on_device(): pl.pallas_call(kernel, out_shape=(jax.ShapeDtypeStruct((BLK, 2 * HALF), B...]
where the time goes in v2:
time: 140 us; the launch traced here: 139 us
  Pallas kernels  133 us (95%)
  local copies, waits for them, and re-layouts  4.91 us (4%)
    pallas_call x1, Pallas kernels, on_device(): pl.pallas_call(kernel, out_shape=(jax.ShapeDtypeStruct((BLK, 2 * HALF), B...  133 us
    unnamed x11, local copies, waits for them, and re-layouts  4.21 us

profile of v2, /device:TPU:16, one launch (start us, length us, event | category | flops | bytes accessed | tf_op | source)
XLA Modules:
  0.0 138.7 jit_solution(15923214070683579464)
XLA Ops:
  0.6 0.0 copy-start.2
  0.6 0.0 copy-start.3
  0.7 0.6 copy-done.2
  1.3 0.0 copy-done.3
  1.4 0.1 copy.15
  1.5 0.1 fusion
  1.6 0.6 reshape.52.table
  2.2 132.9 %shard_map.139 = (bf16[128,3584]{1,0:T(8,128)(2,1)}, f32[27,256]{1,0:T(8,128)}, f32[27,256]{1,0:T(8,128)}) custom-call(bf16[128,4096]{1,0:T(8,128)(2,1)} %tok.1, bf16[64,256]{1,0:T(8,128)(2,1)} %gate_left.1, bf16[16,3584]{1,0:T(8,128)(2,1)} %gate_right.1, bf16[27,256]{1,0:T(8,128)(2,1)} %gate_values.1, s32[27]{0:T(128)} %gate_rows.1, s32[27]{0:T(128)} %gate_cols.1, ...), custom_call_target="tpu_custom_call" | custom-call | tf_op jit(solution)/shard_map/pallas_call | solution.py:526
  135.2 0.0 copy-start.1
  135.2 2.2 %copy.19 = bf16[128,3584]{1,0:T(8,128)(2,1)} copy(bf16[128,3584]{1,0:T(8,128)(2,1)} %get-tuple-element.6) | data formatting | bytes 1835008
  137.3 0.0 copy-done.1
  137.3 0.0 copy-start
  137.4 0.6 copy.20
  138.0 0.2 copy-done
  138.1 0.6 copy.21
  (7 shorter events, 0.0 us)
Async XLA Ops:
  0.6 0.7 copy-start.2
  0.6 0.7 copy-start.3
  135.2 2.2 %copy-start.1 = (f32[27,256]{1,0:T(8,128)S(1)}, f32[27,256]{1,0:T(8,128)}, u32[]{:S(2)}) copy-start(f32[27,256]{1,0:T(8,128)} %get-tuple-element.7) | copy-start | bytes 82948
  137.3 0.8 copy-start

commit v3 on v2

--- a/solution.py
+++ b/solution.py
@@ -17,6 +17,7 @@
 TILE = 256
 PART_A = 768
 ALL = slice(None)
+NEAR, VALUES, FAR = 1, 1, 2
 F32, BF16 = jnp.float32, jnp.bfloat16
 
 
@@ -25,12 +26,13 @@
 
 
 class Net:
-    LATENCY = 3.0
-    RATE = {"x+": 0.045, "x-": 0.045, "z+": 0.045, "z-": 0.045, "y": 0.045, "c": 0.2}
+    LATENCY, WINDOW = 3.0, 5.0
+    RATE = {"x+": 0.045, "x-": 0.045, "z+": 0.045, "z-": 0.045, "y": 0.045, "c": 0.2, "owner": 0.1}
 
     def __init__(self, send_sems, recv_sems):
         self.sems = (send_sems, recv_sems)
         self.now, self.free, self.heap, self.copies, self.spare = 0.0, {}, [], [], []
+        self.waiting, self.asked = {}, 0
 
     def copy(self, src, dst, where):
         i = len(self.copies)
@@ -50,23 +52,36 @@
         self.free[link] = begin + size / self.RATE[link]
         heapq.heappush(self.heap, (self.free[link] + self.LATENCY, len(self.copies), made, then))
 
-    def send(self, src, dst, where, link, size, then):
-        made = self.copy(src, dst, where)
-        made.start()
-        self.track(made, link, size, then)
+    def send(self, src, dst, where, link, size, then, urgency=0):
+        self.asked += 1
+        order = (urgency, self.asked)
+        heapq.heappush(self.waiting.setdefault(link, []), (order, src, dst, where, size, then))
+        self.issue()
+
+    def issue(self):
+        for link, queue in self.waiting.items():
+            while queue and self.free.get(link, 0.0) < self.now + self.WINDOW:
+                _, src, dst, where, size, then = heapq.heappop(queue)
+                made = self.copy(src, dst, where)
+                made.start()
+                self.track(made, link, size, then)
 
     def work(self, cost, do):
         do()
         self.now += cost
+        self.issue()
 
     def run(self):
+        turn = 0
         while self.heap:
             at, _, made, then = heapq.heappop(self.heap)
-            while self.spare and self.now + self.spare[0][0] <= at + 0.5:
+            if self.spare and (turn % 2 or self.now + self.spare[0][0] <= at + 0.5):
                 self.work(*self.spare.pop(0))
+            turn += 1
             self.now = max(self.now, at)
             made.wait_recv()
             then()
+            self.issue()
         while self.spare:
             self.work(*self.spare.pop(0))
 
@@ -85,7 +100,7 @@
             self.then()
 
 
-def ring(net, n, me, axis, block, size, landed, far):
+def ring(net, n, me, axis, block, size, landed, far, urgency):
     reach = n // 2
 
     def step(way, s):
@@ -94,7 +109,7 @@
             return
         ref = block(lax.rem(me - way * (s - 1) + n, n), part)
         to = lax.rem(me + way + n, n)
-        net.send(ref, ref, {axis: to}, axis + ("+" if way == 1 else "-"), size * share, lambda: arrived(way, s))
+        net.send(ref, ref, {axis: to}, axis + ("+" if way == 1 else "-"), size * share, lambda: arrived(way, s), urgency)
 
     def arrived(way, s):
         if s < reach:
@@ -105,9 +120,9 @@
     step(-1, 1)
 
 
-def ring_gather(net, n, me, axis, block, size, done):
+def ring_gather(net, n, me, axis, block, size, done, urgency=0):
     count = Count(n, done)
-    ring(net, n, me, axis, block, size, lambda d: count(), {1: (0, 0.5), -1: (1, 0.5)})
+    ring(net, n, me, axis, block, size, lambda d: count(), {1: (0, 0.5), -1: (1, 0.5)}, urgency)
 
 
 def kernel(
@@ -238,8 +253,8 @@
         lax.fori_loop(first, last, do, 0)
 
     tiles_a, tiles = PART_A // TILE, 2 * HALF // TILE
-    product_a = Count(2, lambda: net.work(1.5, lambda: low_rank(0, tiles_a)))
-    product_b = Count(2, lambda: net.work(5.0, lambda: low_rank(tiles_a, tiles)))
+    product_a = Count(2, lambda: net.work(0.6, lambda: low_rank(0, tiles_a)))
+    product_b = Count(2, lambda: net.work(2.0, lambda: low_rank(tiles_a, tiles)))
 
     def all_ranks():
         product_a()
@@ -248,7 +263,7 @@
     rank_there = Count(7 - 3, all_ranks)
 
     def rank_ready():
-        net.work(2.5, do_rank)
+        net.work(1.0, do_rank)
         share_rank()
 
     left_parts = Count(2 + 1, rank_ready)
@@ -289,14 +304,14 @@
         net.spare.append((0.2, zero_chain))
         for g, rows_ref in ((0, gate_rows), (1, up_rows)):
             for first in range(0, KB, 9):
-                net.spare.append((2.0, lambda a=(g, rows_ref, first, first + 9): sparse(*a)))
+                net.spare.append((0.5, lambda a=(g, rows_ref, first, first + 9): sparse(*a)))
 
     sparse_ready = Count(2, all_sparse)
 
     def tokens_there():
         left_parts()
         for first in range(0, 32, 8):
-            net.spare.append((1.2, lambda a=(first, first + 8): permute_tokens(*a)))
+            net.spare.append((0.4, lambda a=(first, first + 8): permute_tokens(*a)))
         sparse_ready()
 
     def spread_values():
@@ -315,10 +330,10 @@
         return blocks.at[some, pl.ds(pl.multiple_of(i * 16, 16), 16), :]
 
     def values_near():
-        net.work(1.5, spread_values)
-        ring_gather(net, NZ, z, "z", value_slice, 0.221, sparse_ready)
-
-    def gather(near_a, near_b, far_a, far_b):
+        net.work(1.0, spread_values)
+        ring_gather(net, NZ, z, "z", value_slice, 0.221, sparse_ready, VALUES)
+
+    def gather(near_a, near_b, far_a, far_b, urgency):
         counts_a = [Count(2, lambda d=d: far_a(d)) for d in range(NX)]
         counts_b = [Count(2, lambda d=d: far_b(d)) for d in range(NZ)]
 
@@ -326,8 +341,8 @@
             far = {way: (ALL, 1.0), -way: (None, 0.0)}
             ref_a, size_a = near_a
             ref_b, size_b = near_b
-            ring(net, NX, x, "x", lambda i, _: ref_a(i, half), size_a, lambda d: counts_a[d](), far)
-            ring(net, NZ, z, "z", lambda i, _: ref_b(i, half), size_b, lambda d: counts_b[d](), far)
+            ring(net, NX, x, "x", lambda i, _: ref_a(i, half), size_a, lambda d: counts_a[d](), far, urgency)
+            ring(net, NZ, z, "z", lambda i, _: ref_b(i, half), size_b, lambda d: counts_b[d](), far, urgency)
             counts_a[0]()
             counts_b[0]()
 
@@ -335,19 +350,22 @@
 
     def left_gather():
         a, b = slice(0, 32), slice(32, 64)
-
-        def a_far():
-            ring_gather(net, NZ, z, "z", lambda i, h: left.at[:, h, i, a], 0.131, left_parts)
-
-        def b_far():
-            ring_gather(net, NX, x, "x", lambda i, h: left.at[i, h, :, b], 0.262, left_parts)
-
-        all_a, all_b = Count(NX, a_far), Count(NZ, b_far)
+        all_a, all_b = Count(NX, left_parts), Count(NZ, left_parts)
+
+        def a_far(d):
+            i = round_x(d)
+            ring_gather(net, NZ, z, "z", lambda k, h: left.at[i, h, k, a], 0.033, all_a)
+
+        def b_far(d):
+            i = round_z(d)
+            ring_gather(net, NX, x, "x", lambda k, h: left.at[k, h, i, b], 0.033, all_b)
+
         return gather(
             (lambda i, h: left.at[i, h, z, a], 0.016),
             (lambda i, h: left.at[x, h, i, b], 0.016),
-            lambda d: all_a(),
-            lambda d: all_b(),
+            a_far,
+            b_far,
+            0,
         )
 
     def right_gather():
@@ -357,17 +375,18 @@
 
         def a_far(d):
             i = round_x(d)
-            ring_gather(net, NZ, z, "z", lambda k, h: right.at[i, h, k, :, a], size_a, all_a)
+            ring_gather(net, NZ, z, "z", lambda k, h: right.at[i, h, k, :, a], size_a, all_a, FAR)
 
         def b_far(d):
             i = round_z(d)
-            ring_gather(net, NX, x, "x", lambda k, h: right.at[k, h, i, :, b], size_b, all_b)
+            ring_gather(net, NX, x, "x", lambda k, h: right.at[k, h, i, :, b], size_b, all_b, FAR)
 
         return gather(
             (lambda i, h: right.at[i, h, z, :, a], size_a / 2),
             (lambda i, h: right.at[x, h, i, :, b], size_b / 2),
             a_far,
             b_far,
+            NEAR,
         )
 
     swap_left = net.copy(up_left, left.at[x, yl, z], pair)
@@ -396,7 +415,7 @@
         pair,
         "y",
         0.033,
-        lambda: ring_gather(net, NX, x, "x", lambda i, h: shards.at[i, h], 0.066, values_near),
+        lambda: ring_gather(net, NX, x, "x", lambda i, h: shards.at[i, h], 0.066, values_near, 1),
     )
     mine_half = pl.ds(pl.multiple_of(c * 64, 64), 64)
     sent_half = pl.ds(pl.multiple_of(yl * BLK + c * 64, 64), 64)
@@ -436,6 +455,58 @@
     lax.fori_loop(0, 7, gated, 0)
     net.send(back, cols(hidden, yl), pair, "y", 0.459, lambda: None)
 
+    def lot(i):
+        return pl.ds(pl.multiple_of(i * 16, 16), 16)
+
+    def to_owners(g):
+        these = slice(g * KB, (g + 1) * KB)
+        total = grads[these, lot(z), :] + came_up[3, these].astype(F32) + came_down[3, these].astype(F32)
+        mine[g] = total.reshape(KB * 16, BLK)
+        for s in range(8):
+            for p in range(2):
+                parcels[s, g, 0:KB, p * BLK : (p + 1) * BLK] = mine[g, pl.ds(p * 8 + s, KB, stride=16), :]
+        for d in range(NX):
+            for e in range(NL):
+                if d == 0 and e == 0:
+                    continue
+                to_x, to_l = round_x(d), (yl if e == 0 else other)
+                net.send(
+                    parcels.at[to_x * 2 + to_l, g],
+                    arrived_parcels.at[d * 2 + e, g],
+                    {"x": to_x, "yl": to_l},
+                    "owner",
+                    0.033,
+                    lambda: None,
+                )
+
+    def sum_round_z(g):
+        begin, middle, end = g * KB, g * KB + 14, (g + 1) * KB
+        home = Count(2, lambda: to_owners(g))
+
+        def pass_on(way, j):
+            came, leaves = (came_up, leave_up) if way == 1 else (came_down, leave_down)
+            at = lot(round_z(way * (5 - j)))
+            half, rest = (slice(begin, middle), slice(middle, end))[::way]
+            these = half if j == 1 else slice(begin, end)
+            if j == 1:
+                leaves[0, half] = grads[half, at, :].astype(BF16)
+            elif j == 2:
+                leaves[1, half] = (grads[half, at, :] + came[0, half].astype(F32)).astype(BF16)
+                leaves[1, rest] = grads[rest, at, :].astype(BF16)
+            else:
+                leaves[j - 1, these] = (grads[these, at, :] + came[j - 2, these].astype(F32)).astype(BF16)
+            net.send(
+                leaves.at[j - 1, these],
+                came.at[j - 1, these],
+                {"z": round_z(way)},
+                "z+" if way == 1 else "z-",
+                0.055 if j == 1 else 0.11,
+                lambda: home() if j == 4 else pass_on(way, j + 1),
+            )
+
+        pass_on(1, 1)
+        pass_on(-1, 1)
+
     for g, rows_ref, cols_ref in ((0, gate_rows, gate_cols), (1, up_rows, up_cols)):
 
         def gradient(k, _, g=g, rows_ref=rows_ref, cols_ref=cols_ref):
@@ -446,63 +517,14 @@
             return 0
 
         lax.fori_loop(0, KB, gradient, 0)
-
-    def lot(i):
-        return pl.ds(pl.multiple_of(i * 16, 16), 16)
-
-    def exchange():
-        total = grads[:, lot(z), :] + came_up[3].astype(F32) + came_down[3].astype(F32)
-        mine[...] = total.reshape(2 * KB * 16, BLK)
-        for s in range(8):
-            for g in range(2):
-                for p in range(2):
-                    rows = pl.ds(g * KB * 16 + p * 8 + s, KB, stride=16)
-                    parcels[s, g * 32 : g * 32 + KB, p * BLK : (p + 1) * BLK] = mine[rows, :]
-        for d in range(NX):
-            for e in range(NL):
-                if d == 0 and e == 0:
-                    continue
-                to_x, to_l = round_x(d), (yl if e == 0 else other)
-                net.send(
-                    parcels.at[to_x * 2 + to_l],
-                    arrived_parcels.at[d * 2 + e],
-                    {"x": to_x, "yl": to_l},
-                    "x+",
-                    0.065,
-                    lambda: None,
-                )
-
-    home = Count(2, exchange)
-
-    def pass_on(way, j):
-        came, leaves = (came_up, leave_up) if way == 1 else (came_down, leave_down)
-        at = lot(round_z(way * (5 - j)))
-        first, last = (0, 2 * KB) if j > 1 else ((0, KB) if way == 1 else (KB, 2 * KB))
-        if j == 2:
-            half, rest = (slice(0, KB), slice(KB, 2 * KB))[::way]
-            leaves[1, half] = (grads[half, at, :] + came[0, half].astype(F32)).astype(BF16)
-            leaves[1, rest] = grads[rest, at, :].astype(BF16)
-        elif j > 2:
-            leaves[j - 1] = (grads[:, at, :] + came[j - 2].astype(F32)).astype(BF16)
-        else:
-            leaves[0, first:last] = grads[first:last, at, :].astype(BF16)
-        net.send(
-            leaves.at[j - 1, first:last],
-            came.at[j - 1, first:last],
-            {"z": round_z(way)},
-            "z+" if way == 1 else "z-",
-            0.11 if j == 1 else 0.221,
-            lambda: home() if j == 4 else pass_on(way, j + 1),
-        )
-
-    pass_on(1, 1)
-    pass_on(-1, 1)
+        sum_round_z(g)
+        net.now += 1.0
     net.run()
     total = parcels[x * 2 + yl]
     for i in range(1, 8):
         total = total + arrived_parcels[i]
-    out_gate[...] = total[0:KB]
-    out_up[...] = total[32 : 32 + KB]
+    out_gate[...] = total[0, 0:KB]
+    out_up[...] = total[1, 0:KB]
     net.finish()
 
 
@@ -522,7 +544,7 @@
     table = chains(args[5], args[10], base)
     vmem, smem = pl.BlockSpec(memory_space=pltpu.VMEM), pl.BlockSpec(memory_space=pltpu.SMEM)
     specs = [vmem, vmem, vmem, vmem, smem, smem, vmem, vmem, vmem, smem, smem, vmem, smem]
-    copies = 176
+    copies = 240
     return pl.pallas_call(
         kernel,
         out_shape=(
@@ -551,9 +573,9 @@
             pltpu.VMEM((4, 2 * KB, 16, BLK), BF16),
             pltpu.VMEM((4, 2 * KB, 16, BLK), BF16),
             pltpu.VMEM((4, 2 * KB, 16, BLK), BF16),
-            pltpu.VMEM((2 * KB * 16, BLK), F32),
-            pltpu.VMEM((8, 64, 2 * BLK), F32),
-            pltpu.VMEM((8, 64, 2 * BLK), F32),
+            pltpu.VMEM((2, KB * 16, BLK), F32),
+            pltpu.VMEM((8, 2, 32, 2 * BLK), F32),
+            pltpu.VMEM((8, 2, 32, 2 * BLK), F32),
             pltpu.SemaphoreType.DMA((copies,)),
             pltpu.SemaphoreType.DMA((copies,)),
             pltpu.SemaphoreType.DMA((8,)),

time: 140 us -> 129 us (0.921)
  Pallas kernels: 133 us -> 123 us
    pallas_call x1, Pallas kernels: 133 us -> 123 us  [on_device(): pl.pallas_call(kernel, out_shape=(jax.ShapeDtypeStruct((BLK, 2 * HALF), B...]
where the time goes in v3:
time: 129 us
  Pallas kernels  123 us (95%)
  local copies, waits for them, and re-layouts  4.91 us (4%)
    pallas_call x1, Pallas kernels, on_device(): pl.pallas_call(kernel, out_shape=(jax.ShapeDtypeStruct((BLK, 2 * HALF), B...  123 us
    unnamed x11, local copies, waits for them, and re-layouts  4.21 us

profile of v3, /device:TPU:16, one launch (start us, length us, event | category | flops | bytes accessed | tf_op | source)
XLA Modules:
  0.0 128.8 jit_solution(18233066396025654746)
XLA Ops:
  0.6 0.0 copy-start.2
  0.6 0.0 copy-start.3
  0.7 0.6 copy-done.2
  1.3 0.0 copy-done.3
  1.4 0.1 copy.15
  1.5 0.1 fusion
  1.6 0.6 reshape.52.table
  2.2 123.0 %shard_map.139 = (bf16[128,3584]{1,0:T(8,128)(2,1)}, f32[27,256]{1,0:T(8,128)}, f32[27,256]{1,0:T(8,128)}) custom-call(bf16[128,4096]{1,0:T(8,128)(2,1)} %tok.1, bf16[64,256]{1,0:T(8,128)(2,1)} %gate_left.1, bf16[16,3584]{1,0:T(8,128)(2,1)} %gate_right.1, bf16[27,256]{1,0:T(8,128)(2,1)} %gate_values.1, s32[27]{0:T(128)} %gate_rows.1, s32[27]{0:T(128)} %gate_cols.1, ...), custom_call_target="tpu_custom_call" | custom-call | tf_op jit(solution)/shard_map/pallas_call | solution.py:548
  125.2 0.0 copy-start.1
  125.2 2.2 %copy.19 = bf16[128,3584]{1,0:T(8,128)(2,1)} copy(bf16[128,3584]{1,0:T(8,128)(2,1)} %get-tuple-element.6) | data formatting | bytes 1835008
  127.4 0.0 copy-done.1
  127.4 0.0 copy-start
  127.4 0.6 copy.20
  128.0 0.2 copy-done
  128.2 0.6 copy.21
  (7 shorter events, 0.0 us)
Async XLA Ops:
  0.6 0.7 copy-start.2
  0.6 0.7 copy-start.3
  125.2 2.2 %copy-start.1 = (f32[27,256]{1,0:T(8,128)S(1)}, f32[27,256]{1,0:T(8,128)}, u32[]{:S(2)}) copy-start(f32[27,256]{1,0:T(8,128)} %get-tuple-element.7) | copy-start | bytes 82948
  127.4 0.8 copy-start

commit v4 on v3

--- a/solution.py
+++ b/solution.py
@@ -15,9 +15,11 @@
 KB = 27
 HALF = 1792
 TILE = 256
-PART_A = 768
+PARTS = ((0, 512), (512, 1280), (1280, 1792))
+LEFT_A = 16
 ALL = slice(None)
-NEAR, VALUES, FAR = 1, 1, 2
+WIDE, MIDDLE, TIGHT = 50.0, 8.0, 3.0
+NEAR, VALUES, FAR, LATE = 1, 1, 2, 3
 F32, BF16 = jnp.float32, jnp.bfloat16
 
 
@@ -26,13 +28,14 @@
 
 
 class Net:
-    LATENCY, WINDOW = 3.0, 5.0
+    LATENCY = 3.0
     RATE = {"x+": 0.045, "x-": 0.045, "z+": 0.045, "z-": 0.045, "y": 0.045, "c": 0.2, "owner": 0.1}
 
     def __init__(self, send_sems, recv_sems):
         self.sems = (send_sems, recv_sems)
         self.now, self.free, self.heap, self.copies, self.spare = 0.0, {}, [], [], []
         self.waiting, self.asked = {}, 0
+        self.window = {0: WIDE, 1: MIDDLE, 2: TIGHT, 3: TIGHT}
 
     def copy(self, src, dst, where):
         i = len(self.copies)
@@ -60,7 +63,7 @@
 
     def issue(self):
         for link, queue in self.waiting.items():
-            while queue and self.free.get(link, 0.0) < self.now + self.WINDOW:
+            while queue and self.free.get(link, 0.0) < self.now + self.window[queue[0][0][0]]:
                 _, src, dst, where, size, then = heapq.heappop(queue)
                 made = self.copy(src, dst, where)
                 made.start()
@@ -197,8 +200,8 @@
 
     own_rows = pl.ds(pl.multiple_of(yl * BLK, BLK), BLK)
     other_rows = pl.ds(pl.multiple_of(other * BLK, BLK), BLK)
-    keep(cols(gate_right, yl), right.at[x, yl, z, :, 0:HALF])
-    keep(cols(up_right, yl), right.at[x, yl, z, :, HALF : 2 * HALF])
+    keep(cols(gate_right, yl), right.at[x, yl, z, 0])
+    keep(cols(up_right, yl), right.at[x, yl, z, 1])
     keep(tok, t_all.at[own_rows])
     keep(cols(grad_hidden, yl), up_stream.at[own_rows])
     own_left = pltpu.make_async_copy(gate_left, left.at[x, yl, z], local_sems.at[len(keeps)])
@@ -240,61 +243,92 @@
         net.send(ref, ref, across, "y", 0.0, lambda: on(yl, 1 - yh))
         on(yl, yh)
 
-    def low_rank(first, last):
+    def gated(j):
+        for h in range(2):
+            for rows, mine_too in ((other_rows, False), (own_rows, True)):
+                lanes = slice(h * BLK, (h + 1) * BLK)
+                col = j * 2 + h
+                gate = pre[0, rows, lanes] + chain[table[32 + yl * 14 + col], rows, :]
+                up = pre[1, rows, lanes] + chain[28 + table[96 + yl * 14 + col], rows, :]
+                coming = up_stream[rows, pl.ds(pl.multiple_of(col * BLK, BLK), BLK)].astype(F32)
+                sigma = jax.nn.sigmoid(gate)
+                silu = gate * sigma
+                unit = (silu * up).astype(BF16)
+                dpre[col, rows, :] = (coming * up * sigma * (1.0 + gate * (1.0 - sigma))).astype(BF16)
+                dpre[14 + col, rows, :] = (coming * silu).astype(BF16)
+                if mine_too:
+                    hidden[:, pl.ds(pl.multiple_of(yl * HALF + col * BLK, BLK), BLK)] = unit
+                else:
+                    back[:, pl.ds(pl.multiple_of(col * BLK, BLK), BLK)] = unit
+
+    def low_rank_and_gate(first, last):
         def do(j, _):
-            g = (j >= 7).astype(jnp.int32)
             at = pl.ds(pl.multiple_of(j * TILE, TILE), TILE)
-            total = jnp.zeros((2 * BLK, TILE), F32)
-            for i in range(NX):
-                total += dot(rank[g * 4 + i], right[i, :, :, :, at].reshape(TILE, TILE))
-            pre[j] = total
+            for g in range(2):
+                total = jnp.zeros((2 * BLK, TILE), F32)
+                for i in range(NX):
+                    total += dot(rank[g * 4 + i], right[i, :, :, g, :, at].reshape(TILE, TILE))
+                pre[g] = total
+            gated(j)
             return 0
 
         lax.fori_loop(first, last, do, 0)
 
-    tiles_a, tiles = PART_A // TILE, 2 * HALF // TILE
-    product_a = Count(2, lambda: net.work(0.6, lambda: low_rank(0, tiles_a)))
-    product_b = Count(2, lambda: net.work(2.0, lambda: low_rank(tiles_a, tiles)))
+    def part_there(part):
+        first, last = part[0] // TILE, part[1] // TILE
+        for j in range(first, last, 2):
+            end = min(j + 2, last)
+            net.spare.append((0.8 * (end - j), lambda a=(j, end): low_rank_and_gate(*a)))
+
+    part_ready = [Count(3, lambda p=p: part_there(p)) for p in PARTS]
 
     def all_ranks():
-        product_a()
-        product_b()
+        for ready in part_ready:
+            ready()
 
     rank_there = Count(7 - 3, all_ranks)
 
     def rank_ready():
+        net.window.update({2: MIDDLE, 3: MIDDLE})
         net.work(1.0, do_rank)
         share_rank()
 
     left_parts = Count(2 + 1, rank_ready)
 
     def permute_tokens(first, last):
-        def do(r, _):
-            part = t_all[:, pl.ds(pl.multiple_of(r * BLK, BLK), BLK)]
-            new = lax.broadcasted_iota(jnp.int32, (BLK, BLK), 0)
-            old = lax.broadcasted_iota(jnp.int32, (BLK, BLK), 1)
-
-            def source(m):
-                shard = ((m >> 1) & 3) * 16 + (m & 1) * 8 + (m >> 4)
-                return shard * 2 + ((m >> 3) & 1)
-
-            turn = (source(new) == old).astype(F32).astype(BF16)
-            straight = (source(old) == new).astype(F32).astype(BF16)
-            t_perm[r] = dot(part, straight).astype(BF16)
-            t_turn[r] = lax.dot_general(
-                turn, part, (((1,), (1,)), ((), ())), preferred_element_type=F32
-            ).astype(BF16)
+        new = lax.broadcasted_iota(jnp.int32, (BLK, BLK), 0)
+        old = lax.broadcasted_iota(jnp.int32, (BLK, BLK), 1)
+
+        def source(m):
+            shard = ((m >> 1) & 3) * 16 + (m & 1) * 8 + (m >> 4)
+            return shard * 2 + ((m >> 3) & 1)
+
+        turn = (source(new) == old).astype(F32).astype(BF16)
+        straight = (source(old) == new).astype(F32).astype(BF16)
+
+        def do(i, _):
+            for u in range(4):
+                r = i * 4 + u
+                part = t_all[:, pl.ds(pl.multiple_of(r * BLK, BLK), BLK)]
+                t_perm[r] = dot(part, straight).astype(BF16)
+                t_turn[r] = lax.dot_general(
+                    turn, part, (((1,), (1,)), ((), ())), preferred_element_type=F32
+                ).astype(BF16)
             return 0
 
-        lax.fori_loop(first, last, do, 0)
+        lax.fori_loop(first // 4, last // 4, do, 0)
 
     def sparse(g, rows_ref, first, last):
-        def do(k, _):
-            piece = dot(t_perm[rows_ref[k]], blocks[g * KB + k])
-            chain[g * 28 + k + 1] = piece + chain[g * 28 + table[g * 64 + k]]
+        def do(i, _):
+            some = [i * 3 + u for u in range(3)]
+            pieces = [dot(t_perm[rows_ref[k]], blocks[g * KB + k]) for k in some]
+            for k, piece in zip(some, pieces):
+                chain[g * 28 + k + 1] = piece + chain[g * 28 + table[g * 64 + k]]
             return 0
 
-        lax.fori_loop(first, last, do, 0)
+        lax.fori_loop(first // 3, last // 3, do, 0)
+        if g == 1 and last == KB:
+            all_ranks()
 
     def zero_chain():
         chain[0] = jnp.zeros((2 * BLK, BLK), F32)
@@ -333,61 +367,59 @@
         net.work(1.0, spread_values)
         ring_gather(net, NZ, z, "z", value_slice, 0.221, sparse_ready, VALUES)
 
-    def gather(near_a, near_b, far_a, far_b, urgency):
-        counts_a = [Count(2, lambda d=d: far_a(d)) for d in range(NX)]
-        counts_b = [Count(2, lambda d=d: far_b(d)) for d in range(NZ)]
+    def gather(parts):
+        counts = [[Count(2, lambda d=d, f=far: f(d)) for d in range(NX if x_first else NZ)] for x_first, _, _, far, _ in parts]
 
         def begin(half, way):
-            far = {way: (ALL, 1.0), -way: (None, 0.0)}
-            ref_a, size_a = near_a
-            ref_b, size_b = near_b
-            ring(net, NX, x, "x", lambda i, _: ref_a(i, half), size_a, lambda d: counts_a[d](), far, urgency)
-            ring(net, NZ, z, "z", lambda i, _: ref_b(i, half), size_b, lambda d: counts_b[d](), far, urgency)
-            counts_a[0]()
-            counts_b[0]()
+            far_way = {way: (ALL, 1.0), -way: (None, 0.0)}
+            for (x_first, ref, size, _, urgency), count in zip(parts, counts):
+                n, me, axis = (NX, x, "x") if x_first else (NZ, z, "z")
+                ring(net, n, me, axis, lambda i, _, ref=ref: ref(i, half), size, lambda d, t=count: t[d](), far_way, urgency)
+                count[0]()
 
         return (lambda: begin(yl, 1)), (lambda: begin(other, -1))
 
     def left_gather():
-        a, b = slice(0, 32), slice(32, 64)
-        all_a, all_b = Count(NX, left_parts), Count(NZ, left_parts)
-
-        def a_far(d):
-            i = round_x(d)
-            ring_gather(net, NZ, z, "z", lambda k, h: left.at[i, h, k, a], 0.033, all_a)
-
-        def b_far(d):
-            i = round_z(d)
-            ring_gather(net, NX, x, "x", lambda k, h: left.at[k, h, i, b], 0.033, all_b)
-
-        return gather(
-            (lambda i, h: left.at[i, h, z, a], 0.016),
-            (lambda i, h: left.at[x, h, i, b], 0.016),
-            a_far,
-            b_far,
-            0,
-        )
+        parts = []
+        for x_first, rows in ((True, slice(0, LEFT_A)), (False, slice(LEFT_A, 64))):
+            everything = Count(NX if x_first else NZ, left_parts)
+            size = (rows.stop - rows.start) * 0.131 / 128
+
+            def near(i, h, x_first=x_first, rows=rows):
+                return left.at[i, h, z, rows] if x_first else left.at[x, h, i, rows]
+
+            def far(d, x_first=x_first, rows=rows, size=size, everything=everything):
+                if x_first:
+                    i = round_x(d)
+                    ring_gather(net, NZ, z, "z", lambda k, h: left.at[i, h, k, rows], size, everything)
+                else:
+                    i = round_z(d)
+                    ring_gather(net, NX, x, "x", lambda k, h: left.at[k, h, i, rows], size, everything)
+
+            parts.append((x_first, near, size / 2, far, 0))
+        return gather(parts)
 
     def right_gather():
-        a, b = slice(0, PART_A), slice(PART_A, 2 * HALF)
-        size_a, size_b = PART_A * 64e-6, (2 * HALF - PART_A) * 64e-6
-        all_a, all_b = Count(NX, product_a), Count(NZ, product_b)
-
-        def a_far(d):
-            i = round_x(d)
-            ring_gather(net, NZ, z, "z", lambda k, h: right.at[i, h, k, :, a], size_a, all_a, FAR)
-
-        def b_far(d):
-            i = round_z(d)
-            ring_gather(net, NX, x, "x", lambda k, h: right.at[k, h, i, :, b], size_b, all_b, FAR)
-
-        return gather(
-            (lambda i, h: right.at[i, h, z, :, a], size_a / 2),
-            (lambda i, h: right.at[x, h, i, :, b], size_b / 2),
-            a_far,
-            b_far,
-            NEAR,
-        )
+        parts = []
+        for p, (first, last) in enumerate(PARTS):
+            x_first, span = p == 0, slice(first, last)
+            everything = Count(NX if x_first else NZ, part_ready[p])
+            size = (last - first) * 128e-6
+            urgency = FAR if p < 2 else LATE
+
+            def near(i, h, x_first=x_first, span=span):
+                return right.at[i, h, z, :, :, span] if x_first else right.at[x, h, i, :, :, span]
+
+            def far(d, x_first=x_first, span=span, size=size, everything=everything, urgency=urgency):
+                if x_first:
+                    i = round_x(d)
+                    ring_gather(net, NZ, z, "z", lambda k, h: right.at[i, h, k, :, :, span], size, everything, urgency)
+                else:
+                    i = round_z(d)
+                    ring_gather(net, NX, x, "x", lambda k, h: right.at[k, h, i, :, :, span], size, everything, urgency)
+
+            parts.append((x_first, near, size / 2, far, NEAR if p < 2 else VALUES))
+        return gather(parts)
 
     swap_left = net.copy(up_left, left.at[x, yl, z], pair)
 
@@ -405,10 +437,8 @@
     right_own, right_other = right_gather()
     net.track(swap_left, "y", 0.033, left_other)
     swapped_right = Count(2, right_other)
-    net.send(cols(gate_right, other), right.at[x, yl, z, :, 0:HALF], pair, "y", 0.057, swapped_right)
-    net.send(
-        cols(up_right, other), right.at[x, yl, z, :, HALF : 2 * HALF], pair, "y", 0.057, swapped_right
-    )
+    net.send(cols(gate_right, other), right.at[x, yl, z, 0], pair, "y", 0.057, swapped_right)
+    net.send(cols(up_right, other), right.at[x, yl, z, 1], pair, "y", 0.057, swapped_right)
     net.send(
         shards.at[x, yl],
         shards.at[x, yl],
@@ -433,26 +463,6 @@
     right_own()
     net.run()
 
-    def gated(j, _):
-        for h in range(2):
-            for rows, mine_too in ((other_rows, False), (own_rows, True)):
-                lanes = slice(h * BLK, (h + 1) * BLK)
-                col = j * 2 + h
-                gate = pre[j, rows, lanes] + chain[table[32 + yl * 14 + col], rows, :]
-                up = pre[7 + j, rows, lanes] + chain[28 + table[96 + yl * 14 + col], rows, :]
-                coming = up_stream[rows, pl.ds(pl.multiple_of(col * BLK, BLK), BLK)].astype(F32)
-                sigma = jax.nn.sigmoid(gate)
-                silu = gate * sigma
-                unit = (silu * up).astype(BF16)
-                dpre[col, rows, :] = (coming * up * sigma * (1.0 + gate * (1.0 - sigma))).astype(BF16)
-                dpre[14 + col, rows, :] = (coming * silu).astype(BF16)
-                if mine_too:
-                    hidden[:, pl.ds(pl.multiple_of(yl * HALF + col * BLK, BLK), BLK)] = unit
-                else:
-                    back[:, pl.ds(pl.multiple_of(col * BLK, BLK), BLK)] = unit
-        return 0
-
-    lax.fori_loop(0, 7, gated, 0)
     net.send(back, cols(hidden, yl), pair, "y", 0.459, lambda: None)
 
     def lot(i):
@@ -509,14 +519,15 @@
 
     for g, rows_ref, cols_ref in ((0, gate_rows, gate_cols), (1, up_rows, up_cols)):
 
-        def gradient(k, _, g=g, rows_ref=rows_ref, cols_ref=cols_ref):
-            col = cols_ref[k] - (yh * 2 + c) * 28 - yl * 14
-            inside = (col >= 0) & (col < 14)
-            term = dot(t_turn[rows_ref[k]], dpre[g * 14 + jnp.clip(col, 0, 13)])
-            grads[g * KB + k] = jnp.where(inside, term, 0.0)
+        def gradient(i, _, g=g, rows_ref=rows_ref, cols_ref=cols_ref):
+            for k in [i * 3 + u for u in range(3)]:
+                col = cols_ref[k] - (yh * 2 + c) * 28 - yl * 14
+                inside = (col >= 0) & (col < 14)
+                term = dot(t_turn[rows_ref[k]], dpre[g * 14 + jnp.clip(col, 0, 13)])
+                grads[g * KB + k] = jnp.where(inside, term, 0.0)
             return 0
 
-        lax.fori_loop(0, KB, gradient, 0)
+        lax.fori_loop(0, KB // 3, gradient, 0)
         sum_round_z(g)
         net.now += 1.0
     net.run()
@@ -544,7 +555,7 @@
     table = chains(args[5], args[10], base)
     vmem, smem = pl.BlockSpec(memory_space=pltpu.VMEM), pl.BlockSpec(memory_space=pltpu.SMEM)
     specs = [vmem, vmem, vmem, vmem, smem, smem, vmem, vmem, vmem, smem, smem, vmem, smem]
-    copies = 240
+    copies = 320
     return pl.pallas_call(
         kernel,
         out_shape=(
@@ -559,11 +570,11 @@
             pltpu.VMEM((32, 2 * BLK, BLK), BF16),
             pltpu.VMEM((32, BLK, 2 * BLK), BF16),
             pltpu.VMEM((NX, NL, NZ, 64, TILE), BF16),
-            pltpu.VMEM((NX, NL, NZ, 16, 2 * HALF), BF16),
+            pltpu.VMEM((NX, NL, NZ, 2, 16, HALF), BF16),
             pltpu.VMEM((NX, NL, 2, 32, 2 * BLK), BF16),
             pltpu.VMEM((2 * KB, BLK, BLK), BF16),
             pltpu.VMEM((8, 2 * BLK, TILE), BF16),
-            pltpu.VMEM((14, 2 * BLK, TILE), F32),
+            pltpu.VMEM((2, 2 * BLK, TILE), F32),
             pltpu.VMEM((56, 2 * BLK, BLK), F32),
             pltpu.VMEM((2 * BLK, HALF), BF16),
             pltpu.VMEM((28, 2 * BLK, BLK), BF16),

time: 129 us -> 119 us (0.922)
  Pallas kernels: 123 us -> 113 us
    pallas_call x1, Pallas kernels: 123 us -> 113 us  [on_device(): pl.pallas_call(kernel, out_shape=(jax.ShapeDtypeStruct((BLK, 2 * HALF), B...]
where the time goes in v4:
time: 119 us
  Pallas kernels  113 us (95%)
  local copies, waits for them, and re-layouts  4.91 us (4%)
    pallas_call x1, Pallas kernels, on_device(): pl.pallas_call(kernel, out_shape=(jax.ShapeDtypeStruct((BLK, 2 * HALF), B...  113 us
    unnamed x11, local copies, waits for them, and re-layouts  4.21 us

profile of v4, /device:TPU:16, one launch (start us, length us, event | category | flops | bytes accessed | tf_op | source)
XLA Modules:
  0.0 118.9 jit_solution(3791593594682055454)
XLA Ops:
  0.6 0.0 copy-start.2
  0.6 0.0 copy-start.3
  0.7 0.6 copy-done.2
  1.3 0.0 copy-done.3
  1.4 0.1 copy.15
  1.5 0.1 fusion
  1.6 0.6 reshape.52.table
  2.2 113.1 %shard_map.139 = (bf16[128,3584]{1,0:T(8,128)(2,1)}, f32[27,256]{1,0:T(8,128)}, f32[27,256]{1,0:T(8,128)}) custom-call(bf16[128,4096]{1,0:T(8,128)(2,1)} %tok.1, bf16[64,256]{1,0:T(8,128)(2,1)} %gate_left.1, bf16[16,3584]{1,0:T(8,128)(2,1)} %gate_right.1, bf16[27,256]{1,0:T(8,128)(2,1)} %gate_values.1, s32[27]{0:T(128)} %gate_rows.1, s32[27]{0:T(128)} %gate_cols.1, ...), custom_call_target="tpu_custom_call" | custom-call | tf_op jit(solution)/shard_map/pallas_call | solution.py:559
  115.3 0.0 copy-start.1
  115.3 2.2 %copy.19 = bf16[128,3584]{1,0:T(8,128)(2,1)} copy(bf16[128,3584]{1,0:T(8,128)(2,1)} %get-tuple-element.6) | data formatting | bytes 1835008
  117.5 0.0 copy-done.1
  117.5 0.0 copy-start
  117.5 0.6 copy.20
  118.1 0.2 copy-done
  118.2 0.6 copy.21
  (7 shorter events, 0.0 us)
Async XLA Ops:
  0.6 0.7 copy-start.2
  0.6 0.7 copy-start.3
  115.3 2.2 %copy-start.1 = (f32[27,256]{1,0:T(8,128)S(1)}, f32[27,256]{1,0:T(8,128)}, u32[]{:S(2)}) copy-start(f32[27,256]{1,0:T(8,128)} %get-tuple-element.7) | copy-start | bytes 82948
  117.5 0.8 copy-start

commit v5 on v4

--- a/solution.py
+++ b/solution.py
@@ -431,7 +431,8 @@
     def _():
         net.copy(gate_left, left.at[x, yl, z], pair).start()
 
-    for made in keeps:
+    at_first = (keeps[0], keeps[1], keeps[4])
+    for made in at_first:
         made.wait()
     left_own, left_other = left_gather()
     right_own, right_other = right_gather()
@@ -461,6 +462,8 @@
     net.send(cols(grad_hidden, other), up_stream.at[own_rows], pair, "y", 0.459, lambda: None)
     left_own()
     right_own()
+    for made in keeps[2:4]:
+        made.wait()
     net.run()
 
     net.send(back, cols(hidden, yl), pair, "y", 0.459, lambda: None)
@@ -554,7 +557,8 @@
     base = (lax.axis_index("yh") * 2 + lax.axis_index("c")) * 28
     table = chains(args[5], args[10], base)
     vmem, smem = pl.BlockSpec(memory_space=pltpu.VMEM), pl.BlockSpec(memory_space=pltpu.SMEM)
-    specs = [vmem, vmem, vmem, vmem, smem, smem, vmem, vmem, vmem, smem, smem, vmem, smem]
+    hbm = pl.BlockSpec(memory_space=pl.ANY)
+    specs = [hbm, hbm, hbm, vmem, smem, smem, hbm, hbm, vmem, smem, smem, hbm, smem]
     copies = 320
     return pl.pallas_call(
         kernel,

time: 119 us -> 119 us (level)
  no operation moved by 1% of the time
where the time goes in v5:
time: 119 us; the launch traced here: 118 us
  Pallas kernels  112 us (94%)
  local copies, waits for them, and re-layouts  4.91 us (4%)
    pallas_call x1, Pallas kernels, on_device(): pl.pallas_call(kernel, out_shape=(jax.ShapeDtypeStruct((BLK, 2 * HALF), B...  112 us
    unnamed x11, local copies, waits for them, and re-layouts  4.21 us

profile of v5, /device:TPU:16, one launch (start us, length us, event | category | flops | bytes accessed | tf_op | source)
XLA Modules:
  0.0 118.3 jit_solution(1243562667819794822)
XLA Ops:
  0.6 0.0 copy-start.2
  0.6 0.0 copy-start.3
  0.7 0.6 copy-done.2
  1.3 0.0 copy-done.3
  1.4 0.1 copy.15
  1.5 0.1 fusion
  1.6 0.6 reshape.52.table
  2.2 112.5 %shard_map.139 = (bf16[128,3584]{1,0:T(8,128)(2,1)}, f32[27,256]{1,0:T(8,128)}, f32[27,256]{1,0:T(8,128)}) custom-call(bf16[128,4096]{1,0:T(8,128)(2,1)} %tok.1, bf16[64,256]{1,0:T(8,128)(2,1)} %gate_left.1, bf16[16,3584]{1,0:T(8,128)(2,1)} %gate_right.1, bf16[27,256]{1,0:T(8,128)(2,1)} %gate_values.1, s32[27]{0:T(128)} %gate_rows.1, s32[27]{0:T(128)} %gate_cols.1, ...), custom_call_target="tpu_custom_call" | custom-call | tf_op jit(solution)/shard_map/pallas_call | solution.py:563
  114.7 0.0 copy-start.1
  114.7 2.2 %copy.19 = bf16[128,3584]{1,0:T(8,128)(2,1)} copy(bf16[128,3584]{1,0:T(8,128)(2,1)} %get-tuple-element.6) | data formatting | bytes 1835008
  116.9 0.0 copy-done.1
  116.9 0.0 copy-start
  116.9 0.6 copy.20
  117.5 0.2 copy-done
  117.7 0.6 copy.21
  (7 shorter events, 0.0 us)
Async XLA Ops:
  0.6 0.7 copy-start.2
  0.6 0.7 copy-start.3
  114.7 2.2 %copy-start.1 = (f32[27,256]{1,0:T(8,128)S(1)}, f32[27,256]{1,0:T(8,128)}, u32[]{:S(2)}) copy-start(f32[27,256]{1,0:T(8,128)} %get-tuple-element.7) | copy-start | bytes 82948
  116.9 0.8 copy-start

commit v6 on v5

--- a/solution.py
+++ b/solution.py
@@ -523,14 +523,14 @@
     for g, rows_ref, cols_ref in ((0, gate_rows, gate_cols), (1, up_rows, up_cols)):
 
         def gradient(i, _, g=g, rows_ref=rows_ref, cols_ref=cols_ref):
-            for k in [i * 3 + u for u in range(3)]:
+            for k in [i * 9 + u for u in range(9)]:
                 col = cols_ref[k] - (yh * 2 + c) * 28 - yl * 14
                 inside = (col >= 0) & (col < 14)
                 term = dot(t_turn[rows_ref[k]], dpre[g * 14 + jnp.clip(col, 0, 13)])
                 grads[g * KB + k] = jnp.where(inside, term, 0.0)
             return 0
 
-        lax.fori_loop(0, KB // 3, gradient, 0)
+        lax.fori_loop(0, KB // 9, gradient, 0)
         sum_round_z(g)
         net.now += 1.0
     net.run()

time: 119 us -> 117 us (0.983)
    pallas_call x1, Pallas kernels: 112 us -> 111 us  [on_device(): pl.pallas_call(kernel, out_shape=(jax.ShapeDtypeStruct((BLK, 2 * HALF), B...]
where the time goes in v6:
time: 117 us
  Pallas kernels  111 us (95%)
  local copies, waits for them, and re-layouts  4.91 us (4%)
    pallas_call x1, Pallas kernels, on_device(): pl.pallas_call(kernel, out_shape=(jax.ShapeDtypeStruct((BLK, 2 * HALF), B...  111 us
    unnamed x11, local copies, waits for them, and re-layouts  4.21 us

profile of v6, /device:TPU:16, one launch (start us, length us, event | category | flops | bytes accessed | tf_op | source)
XLA Modules:
  0.0 117.1 jit_solution(830001459557437330)
XLA Ops:
  0.6 0.0 copy-start.2
  0.6 0.0 copy-start.3
  0.7 0.6 copy-done.2
  1.3 0.0 copy-done.3
  1.4 0.1 copy.15
  1.5 0.1 fusion
  1.6 0.6 reshape.52.table
  2.2 111.3 %shard_map.139 = (bf16[128,3584]{1,0:T(8,128)(2,1)}, f32[27,256]{1,0:T(8,128)}, f32[27,256]{1,0:T(8,128)}) custom-call(bf16[128,4096]{1,0:T(8,128)(2,1)} %tok.1, bf16[64,256]{1,0:T(8,128)(2,1)} %gate_left.1, bf16[16,3584]{1,0:T(8,128)(2,1)} %gate_right.1, bf16[27,256]{1,0:T(8,128)(2,1)} %gate_values.1, s32[27]{0:T(128)} %gate_rows.1, s32[27]{0:T(128)} %gate_cols.1, ...), custom_call_target="tpu_custom_call" | custom-call | tf_op jit(solution)/shard_map/pallas_call | solution.py:563
  113.5 0.0 copy-start.1
  113.5 2.2 %copy.19 = bf16[128,3584]{1,0:T(8,128)(2,1)} copy(bf16[128,3584]{1,0:T(8,128)(2,1)} %get-tuple-element.6) | data formatting | bytes 1835008
  115.7 0.0 copy-done.1
  115.7 0.0 copy-start
  115.7 0.6 copy.20
  116.3 0.2 copy-done
  116.5 0.6 copy.21
  (7 shorter events, 0.0 us)
Async XLA Ops:
  0.6 0.7 copy-start.2
  0.6 0.7 copy-start.3
  113.5 2.2 %copy-start.1 = (f32[27,256]{1,0:T(8,128)S(1)}, f32[27,256]{1,0:T(8,128)}, u32[]{:S(2)}) copy-start(f32[27,256]{1,0:T(8,128)} %get-tuple-element.7) | copy-start | bytes 82948
  115.7 0.8 copy-start
